TPU v7x, 256 devices: a whole 4x4x8 slice. The times are simulated.
256 devices in a mesh: rep: 16 (over x, z_hi), tp: 16 (over z_lo, y, core).
Axes of the slice: x: 4, y: 4, z: 8 (z_hi: 4, z_lo: 2; z = z_hi * 2 + z_lo), core: 2. Of those that a mesh axis runs over, the one named last changes fastest.
Arguments:
- hidden: bfloat16 [32768, 8192], P('rep', 'tp'), may hold values from -0.0625 to 0.0625
- target: bfloat16 [32768, 1024], P('rep'), may hold values from -6 to 6
- inner_weight: bfloat16 [16, 8192, 1024], P('rep', 'tp'), as said below
- first_moment: float32 [16, 8192, 1024], P('rep', 'tp'), may hold values from -1.5 to 1.5
- second_moment: float32 [16, 8192, 1024], P('rep', 'tp'), may hold values from 0.001 to 0.01
- anchor: float32 [16, 512, 1024], P('tp', 'rep')
- outer_momentum: float32 [16, 512, 1024], P('tp', 'rep'), may hold values from -1.5 to 1.5
Outputs:
- fragment: bfloat16 [8192, 1024], P('tp')
- momentum_new: float32 [16, 512, 1024], P('tp', 'rep')
Inputs may be any that keep to these rules, and one draw needn't show every extreme that they name: `inner_weight`: each replica's inner weights are the anchor plus a drift of their own.
All inputs are finite; a program needn't handle non-finite values.
Results may differ from a plain program's by a relative error of at most 0.0017.
Values may be sent and summed in bfloat16 or wider, within the bound.
No kernel may reach another device: no remote copies, remote signals or barrier semaphores. Data moves between devices by JAX's collectives and lax.ppermute only.
A program may use at most 64 MiB of HBM per device.

v0:
```python
import jax
import jax.numpy as jnp
from jax import lax
from jax.sharding import PartitionSpec as P

beta_one = 0.9
beta_two = 0.999
inner_rate = 0.2
decay_rate = 0.1
outer_rate = 0.7
outer_mu = 0.9
adam_eps = 1e-08


def local(hidden, target, inner_weight, first_moment, second_moment, anchor, outer_momentum):
    weight = inner_weight[0]
    partial_value = jnp.dot(hidden, weight, preferred_element_type=jnp.float32)
    summed = lax.psum_scatter(
        partial_value.astype(jnp.bfloat16), "tp", scatter_dimension=0, tiled=True
    ).astype(jnp.float32)
    count = summed.shape[0]
    goal = lax.dynamic_slice_in_dim(target, lax.axis_index("tp") * count, count, 0)
    residual = (summed - goal.astype(jnp.float32)).astype(jnp.bfloat16)
    grad = lax.dot_general(
        hidden,
        lax.all_gather(residual, "tp", axis=0, tiled=True),
        (((0,), (0,)), ((), ())),
        preferred_element_type=jnp.float32,
    )
    moment_one = beta_one * first_moment[0] + (1.0 - beta_one) * grad
    moment_two = beta_two * second_moment[0] + (1.0 - beta_two) * grad * grad
    corr_one = 1.0 - beta_one**3
    corr_two = 1.0 - beta_two**3
    weight_f = weight.astype(jnp.float32)
    step_dir = moment_one / corr_one / (jnp.sqrt(moment_two / corr_two) + adam_eps)
    updated = weight_f - inner_rate * (step_dir + decay_rate * weight_f)
    replicas = lax.axis_size("rep")
    replica_mean = lax.psum_scatter(updated, "rep", scatter_dimension=0, tiled=True) / replicas
    anchor_rows = anchor[0]
    delta = anchor_rows - replica_mean
    momentum_new = outer_mu * outer_momentum[0] + delta
    piece = (anchor_rows - outer_rate * (delta + outer_mu * momentum_new)).astype(jnp.bfloat16)
    fragment = lax.all_gather(piece, "rep", axis=0, tiled=True)
    return (fragment, momentum_new[None])


def solution(mesh):
    placed = (
        P("rep", "tp"),
        P("rep", None),
        P("rep", "tp", None),
        P("rep", "tp", None),
        P("rep", "tp", None),
        P("tp", "rep", None),
        P("tp", "rep", None),
    )
    return jax.shard_map(
        local,
        mesh=mesh,
        in_specs=placed,
        out_specs=(P("tp", None), P("tp", "rep", None)),
        check_vma=False,
    )
```

profile of v0, /device:TPU:8, one launch (start us, length us, event | category | flops | bytes accessed | tf_op | source)
XLA Modules:
  0.0 292.7 jit_solution(12165705362500873506)
XLA Ops:
  7.2 0.0 copy-start
  7.2 0.0 reduce-scatter.5.cloned.1.call-start
  7.2 1.5 copy-done
  8.8 5.5 %convolution_convert_fusion = bf16[2048,1024]{1,0:T(8,128)(2,1)} fusion(bf16[2048,512]{1,0:T(8,128)(2,1)S(1)} %copy-done, bf16[1,512,1024]{2,1,0:T(8,128)(2,1)} %param.9), kind=kOutput, calls=%fused_computation | convolution fusion | flops 2149580800 | bytes 7340032 | tf_op jit(solution)/shard_map/dot_general | solution.py:17
  14.3 0.0 reduce-scatter.5.cloned.1.call-update
  14.3 0.0 all-gather.3.cloned.1.call-start
  14.4 68.8 %reduce-scatter.5.cloned.1.call-done = bf16[128,1024]{1,0:T(8,128)(2,1)} async-done(((bf16[2048,1024]{1,0:T(8,128)(2,1)}), bf16[128,1024]{1,0:T(8,128)(2,1)}) %reduce-scatter.5.cloned.1.call-update) | async-done | bytes 262160 | tf_op jit(solution)/shard_map/reduce_scatter | solution.py:18
  83.2 1.8 subtract_convert_fusion
  85.0 0.0 all-gather.3.cloned.1.call-update
  85.1 0.0 reduce-scatter.7.cloned.1.call-start
  85.1 0.0 copy-done.1
  85.1 1.3 copy.17
  86.4 2.9 copy.18
  89.3 3.0 %copy.19 = f32[1,512,1024]{1,2,0:T(8,128)} copy(f32[1,512,1024]{2,1,0:T(8,128)} %param.11) | data formatting | bytes 4194304 | tf_op args[4]
  92.4 34.4 %all-gather.3.cloned.1.call-done = bf16[2048,1024]{1,0:T(8,128)(2,1)} async-done(((bf16[128,1024]{1,0:T(8,128)(2,1)}), bf16[2048,1024]{1,0:T(8,128)(2,1)}) %all-gather.3.cloned.1.call-update) | async-done | bytes 4194320 | tf_op jit(solution)/shard_map/all_gather | solution.py:26
  126.8 0.0 copy-done.2
  126.8 8.6 %convert_subtract_fusion = f32[512,1024]{0,1:T(8,128)} fusion(f32[1,512,1024]{1,2,0:T(8,128)} %copy.19, f32[1,512,1024]{1,2,0:T(8,128)} %copy.18, bf16[2048,1024]{1,0:T(8,128)(2,1)} %all-gather.3.cloned.1.call-done, bf16[2048,512]{1,0:T(8,128)(2,1)S(1)} %copy-done, bf16[1,512,1024]{1,2,0:T(8,128)(2,1)S(1)} %copy-done.2), kind=kOutput, calls=%fused_computation.2 | convolution fusion | flops 2155872256 | bytes 13631488 | tf_op jit(solution)/shard_map/dot_general | solution.py:24
  135.3 2.9 copy.23
  138.3 0.0 reduce-scatter.7.cloned.1.call-update
  138.3 0.0 all-gather.5.cloned.1.call-start
  138.3 0.8 copy-done.3
  139.2 0.2 copy.16
  139.4 0.0 copy-done.4
  139.4 1.0 copy.20
  140.4 88.4 %reduce-scatter.7.cloned.1.call-done = f32[32,1024]{1,0:T(8,128)} async-done(((f32[512,1024]{1,0:T(8,128)}), f32[32,1024]{1,0:T(8,128)}) %reduce-scatter.7.cloned.1.call-update) | async-done | bytes 131088
  228.8 1.9 copy.24
  230.7 1.4 fusion.11
  232.1 0.8 copy.21
  232.8 0.0 all-gather.5.cloned.1.call-update
  232.9 0.8 copy.22
  233.7 50.2 %all-gather.5.cloned.1.call-done = bf16[512,1024]{1,0:T(8,128)(2,1)} async-done(((bf16[32,1024]{1,0:T(8,128)(2,1)}), bf16[512,1024]{1,0:T(8,128)(2,1)}) %all-gather.5.cloned.1.call-update) | async-done | bytes 1048592 | tf_op jit(solution)/shard_map/all_gather | solution.py:43
  283.9 2.3 copy.26
  (4 shorter events, 0.0 us)
Async XLA Ops:
  7.2 1.6 copy-start
  7.2 76.0 %reduce-scatter.5.cloned.1.call-start = ((), (), s32[]{:S(2)}) async-start(), calls=%async_computation.2 | async-start | bytes 4456448 | tf_op jit(solution)/shard_map/reduce_scatter | solution.py:18
  14.3 70.8 %copy-start.1 = (bf16[1,512,1024]{2,1,0:T(8,128)(2,1)S(1)}, bf16[1,512,1024]{2,1,0:T(8,128)(2,1)}, u32[]{:S(2)}) copy-start(bf16[1,512,1024]{2,1,0:T(8,128)(2,1)} %param.9) | copy-start | bytes 3145732
  14.3 112.5 %all-gather.3.cloned.1.call-start = ((), (), s32[]{:S(2)}) async-start(), calls=%async_computation.3 | async-start | bytes 4456448 | tf_op jit(solution)/shard_map/all_gather | solution.py:26
  85.1 143.8 %reduce-scatter.7.cloned.1.call-start = ((), (), s32[]{:S(2)}) async-start(), calls=%async_computation.5 | async-start | bytes 2228224
  89.3 37.4 %copy-start.2 = (bf16[1,512,1024]{1,2,0:T(8,128)(2,1)S(1)}, bf16[1,512,1024]{1,2,0:T(8,128)(2,1)}, u32[]{:S(2)}) copy-start(bf16[1,512,1024]{1,2,0:T(8,128)(2,1)} %copy.17) | copy-start | bytes 3145732
  138.3 0.9 copy-start.3
  138.3 1.1 copy-start.4
  138.3 145.6 %all-gather.5.cloned.1.call-start = ((), (), s32[]{:S(2)}) async-start(), calls=%async_computation.4 | async-start | bytes 1114112 | tf_op jit(solution)/shard_map/all_gather | solution.py:43
Sparse Core Ops, SparseCore 0:
  14.4 68.7 reduce-scatter.4
  85.2 41.5 all-gather.2
  138.4 90.3 reduce-scatter.6
  233.0 50.9 all-gather.4
where the time goes:
time: 293 us
  waiting for transfers between devices  242 us (83%)
  local copies, waits for them, and re-layouts  19.5 us (7%)
  matrix products  14.1 us (5%)
  between operations  13.8 us (5%)
  other arithmetic  3.19 us (1%)
    unnamed x5, waiting for transfers between devices  88.5 us
    reduce_scatter x1, waiting for transfers between devices, local(): lax.psum_scatter(partial_value.astype(jnp.bfloat16), 'tp', scatter_dimens...  68.8 us
    all_gather x1, waiting for transfers between devices, local(): fragment = lax.all_gather(piece, 'rep', axis=0, tiled=True)  50.2 us
    all_gather x1, waiting for transfers between devices, local(): lax.all_gather(residual, 'tp', axis=0, tiled=True)  34.4 us
    unnamed x19, local copies, waits for them, and re-layouts  18.7 us
    dot_general x1, matrix products, local(): lax.dot_general(hidden, lax.all_gather(residual, 'tp', axis=0, tiled=True...  8.58 us
  transfers between devices with their start and end apart: 4, of which 4 were waited for; matrix products, arithmetic and copies ran while one was open for 3% of the time, Pallas kernels for 0%

commit v1 on v0

--- a/solution.py
+++ b/solution.py
@@ -23,7 +23,9 @@
     residual = (summed - goal.astype(jnp.float32)).astype(jnp.bfloat16)
     grad = lax.dot_general(
         hidden,
-        lax.all_gather(residual, "tp", axis=0, tiled=True),
+        jnp.concatenate(
+            lax.all_to_all(jnp.stack([residual] * lax.axis_size("tp")), "tp", 0, 0), axis=0
+        ),
         (((0,), (0,)), ((), ())),
         preferred_element_type=jnp.float32,
     )

time: 293 us -> 323 us (1.10)
  waiting for transfers between devices: 242 us -> 261 us
  starting transfers between devices: 0.16 us -> 9.15 us
    all_to_all x0 -> x1, waiting for transfers between devices: none -> 52.5 us  [local(): lax.all_to_all(jnp.stack([residual] * lax.axis_size('tp')), 'tp', 0, 0)]
    all_gather x1 -> x0, waiting for transfers between devices: 34.4 us -> none  [local(): lax.all_gather(residual, 'tp', axis=0, tiled=True)]
    all_to_all x0 -> x1, starting transfers between devices: none -> 9.03 us  [local(): lax.all_to_all(jnp.stack([residual] * lax.axis_size('tp')), 'tp', 0, 0)]
    unnamed x5 -> x4, waiting for transfers between devices: 88.5 us -> 89.6 us
where the time goes in v1:
time: 323 us
  waiting for transfers between devices  261 us (81%)
  local copies, waits for them, and re-layouts  22 us (7%)
  matrix products  14.1 us (4%)
  between operations  13.8 us (4%)
  starting transfers between devices  9.15 us (3%)
    unnamed x4, waiting for transfers between devices  89.6 us
    reduce_scatter x1, waiting for transfers between devices, local(): lax.psum_scatter(partial_value.astype(jnp.bfloat16), 'tp', scatter_dimens...  68.9 us
    all_to_all x1, waiting for transfers between devices, local(): lax.all_to_all(jnp.stack([residual] * lax.axis_size('tp')), 'tp', 0, 0)  52.5 us
    all_gather x1, waiting for transfers between devices, local(): fragment = lax.all_gather(piece, 'rep', axis=0, tiled=True)  50.3 us
    unnamed x19, local copies, waits for them, and re-layouts  18.7 us
    all_to_all x1, starting transfers between devices, local(): lax.all_to_all(jnp.stack([residual] * lax.axis_size('tp')), 'tp', 0, 0)  9.03 us
    dot_general x1, matrix products, local(): lax.dot_general(hidden, jnp.concatenate(lax.all_to_all(jnp.stack([residua...  8.57 us
  transfers between devices with their start and end apart: 4, of which 4 were waited for; matrix products, arithmetic and copies ran while one was open for 3% of the time, Pallas kernels for 0%

profile of v1, /device:TPU:8, one launch (start us, length us, event | category | flops | bytes accessed | tf_op | source)
XLA Modules:
  0.0 322.7 jit_solution(13245996481023785322)
XLA Ops:
  7.2 0.0 copy-start
  7.2 0.0 reduce-scatter.5.cloned.1.call-start
  7.2 1.5 copy-done
  8.8 5.5 %convolution_convert_fusion = bf16[2048,1024]{1,0:T(8,128)(2,1)} fusion(bf16[2048,512]{1,0:T(8,128)(2,1)S(1)} %copy-done, bf16[1,512,1024]{2,1,0:T(8,128)(2,1)} %param.9), kind=kOutput, calls=%fused_computation | convolution fusion | flops 2149580800 | bytes 7340032 | tf_op jit(solution)/shard_map/dot_general | solution.py:17
  14.3 0.0 reduce-scatter.5.cloned.1.call-update
  14.3 68.9 %reduce-scatter.5.cloned.1.call-done = bf16[128,1024]{1,0:T(8,128)(2,1)} async-done(((bf16[2048,1024]{1,0:T(8,128)(2,1)}), bf16[128,1024]{1,0:T(8,128)(2,1)}) %reduce-scatter.5.cloned.1.call-update) | async-done | bytes 262160 | tf_op jit(solution)/shard_map/reduce_scatter | solution.py:18
  83.2 1.1 subtract_convert_fusion
  84.3 2.5 stack.2
  86.8 9.0 %all-to-all-start = ((bf16[16,128,1024]{2,1,0:T(8,128)(2,1)}), bf16[16,128,1024]{2,1,0:T(8,128)(2,1)}, u32[]{:S(2)}, u32[]{:S(2)}) async-start(bf16[16,128,1024]{2,1,0:T(8,128)(2,1)} %stack.2), calls=%async_computation.1 | async-start | bytes 8388608 | tf_op jit(solution)/shard_map/all_to_all | solution.py:27
  95.8 0.0 reduce-scatter.7.cloned.1.call-start
  95.9 0.0 copy-done.1
  95.9 1.3 copy.17
  97.2 2.9 copy.18
  100.2 3.0 copy.19
  103.1 52.5 %all-to-all-done = bf16[16,128,1024]{2,1,0:T(8,128)(2,1)} async-done(((bf16[16,128,1024]{2,1,0:T(8,128)(2,1)}), bf16[16,128,1024]{2,1,0:T(8,128)(2,1)}, u32[]{:S(2)}, u32[]{:S(2)}) %all-to-all-start) | async-done | bytes 4194336 | tf_op jit(solution)/shard_map/all_to_all | solution.py:27
  155.6 0.0 copy-done.2
  155.6 8.6 %convert_subtract_fusion = f32[512,1024]{0,1:T(8,128)} fusion(f32[1,512,1024]{1,2,0:T(8,128)} %copy.19, f32[1,512,1024]{1,2,0:T(8,128)} %copy.18, bf16[2048,1024]{1,0:T(8,128)(2,1)} %bitcast.3, bf16[2048,512]{1,0:T(8,128)(2,1)S(1)} %copy-done, bf16[1,512,1024]{1,2,0:T(8,128)(2,1)S(1)} %copy-done.2), kind=kOutput, calls=%fused_computation.2 | convolution fusion | flops 2155872256 | bytes 13631488 | tf_op jit(solution)/shard_map/dot_general | solution.py:24
  164.2 2.9 copy.23
  167.1 0.0 reduce-scatter.7.cloned.1.call-update
  167.1 0.0 all-gather.2.cloned.1.call-start
  167.2 0.8 copy-done.3
  168.0 0.2 copy.16
  168.2 0.0 copy-done.4
  168.2 1.0 copy.20
  169.2 89.5 %reduce-scatter.7.cloned.1.call-done = f32[32,1024]{1,0:T(8,128)} async-done(((f32[512,1024]{1,0:T(8,128)}), f32[32,1024]{1,0:T(8,128)}) %reduce-scatter.7.cloned.1.call-update) | async-done | bytes 131088
  258.7 1.9 copy.24
  260.6 1.4 fusion.11
  262.0 0.8 copy.21
  262.8 0.0 all-gather.2.cloned.1.call-update
  262.8 0.8 copy.22
  263.6 50.3 %all-gather.2.cloned.1.call-done = bf16[512,1024]{1,0:T(8,128)(2,1)} async-done(((bf16[32,1024]{1,0:T(8,128)(2,1)}), bf16[512,1024]{1,0:T(8,128)(2,1)}) %all-gather.2.cloned.1.call-update) | async-done | bytes 1048592 | tf_op jit(solution)/shard_map/all_gather | solution.py:45
  313.9 2.3 copy.26
  (4 shorter events, 0.0 us)
Async XLA Ops:
  7.2 1.6 copy-start
  7.2 76.0 %reduce-scatter.5.cloned.1.call-start = ((), (), s32[]{:S(2)}) async-start(), calls=%async_computation.3 | async-start | bytes 4456448 | tf_op jit(solution)/shard_map/reduce_scatter | solution.py:18
  86.8 9.1 %copy-start.1 = (bf16[1,512,1024]{2,1,0:T(8,128)(2,1)S(1)}, bf16[1,512,1024]{2,1,0:T(8,128)(2,1)}, u32[]{:S(2)}) copy-start(bf16[1,512,1024]{2,1,0:T(8,128)(2,1)} %param.9) | copy-start | bytes 3145732
  86.8 68.8 %all-to-all-start = ((bf16[16,128,1024]{2,1,0:T(8,128)(2,1)}), bf16[16,128,1024]{2,1,0:T(8,128)(2,1)}, u32[]{:S(2)}, u32[]{:S(2)}) async-start(bf16[16,128,1024]{2,1,0:T(8,128)(2,1)} %stack.2), calls=%async_computation.1 | async-start | bytes 8388608 | tf_op jit(solution)/shard_map/all_to_all | solution.py:27
  95.8 162.9 %reduce-scatter.7.cloned.1.call-start = ((), (), s32[]{:S(2)}) async-start(), calls=%async_computation.5 | async-start | bytes 2228224
  100.2 55.5 %copy-start.2 = (bf16[1,512,1024]{1,2,0:T(8,128)(2,1)S(1)}, bf16[1,512,1024]{1,2,0:T(8,128)(2,1)}, u32[]{:S(2)}) copy-start(bf16[1,512,1024]{1,2,0:T(8,128)(2,1)} %copy.17) | copy-start | bytes 3145732
  167.1 0.9 copy-start.3
  167.1 1.1 copy-start.4
  167.1 146.8 %all-gather.2.cloned.1.call-start = ((), (), s32[]{:S(2)}) async-start(), calls=%async_computation.4 | async-start | bytes 1114112 | tf_op jit(solution)/shard_map/all_gather | solution.py:45
Sparse Core Ops, SparseCore 0:
  14.4 68.7 reduce-scatter.4
  167.2 91.4 reduce-scatter.6
  262.9 50.9 all-gather.1
